TPU v7x, 256 devices: a whole 4x4x8 slice. The times are simulated.
256 devices in a mesh: energy: 64 (over x, z_hi, y), space: 4 (over z_lo, core).
Axes of the slice: x: 4, y: 4, z: 8 (z_hi: 4, z_lo: 2; z = z_hi * 2 + z_lo), core: 2. Of those that a mesh axis runs over, the one named last changes fastest.
Arguments:
- g_lesser: bfloat16 [64, 2, 4, 512, 512], P('energy', None, 'space'), may hold values from -6 to 6, as said below
- w_lesser: bfloat16 [64, 2, 4, 512, 512], P('energy', None, 'space'), may hold values from -6 to 6, as said below
- g_retarded: bfloat16 [64, 2, 4, 4, 512, 512], P('energy', None, 'space'), may hold values from -0.1875 to 0.1875
- energy_index: int32 [64], replicated, may hold values from 0 to 63, each once
Outputs:
- sigma_lesser: bfloat16 [64, 2, 4, 512, 512], P('energy', None, 'space')
- delta_green: bfloat16 [64, 2, 4, 512, 512], P('energy', None, 'space')
Inputs may be any that keep to these rules, and one draw needn't show every extreme that they name: `g_lesser`: anti-Hermitian in every diagonal block at every energy: element (j, i) of component 0 is minus element (i, j), of component 1 equal to it. `w_lesser`: anti-Hermitian in every diagonal block at every energy: element (j, i) of component 0 is minus element (i, j), of component 1 equal to it. `energy_index`: each grid point once.
All inputs are finite; a program needn't handle non-finite values.
Results may differ from a plain program's by a relative error of at most 0.013.
Values may be sent and summed in bfloat16 or wider, within the bound.
A program may use at most 128 MiB of HBM per device.

v0:
```python
import math
import jax
import jax.numpy as jnp
from jax import lax
from jax.sharding import PartitionSpec as P


def twiddles(energy_index, per_device, groups):
    grid_size = energy_index.shape[0]
    padded_len = 2 * grid_size
    row_count = 2 * grid_size
    row_ids = lax.iota(jnp.int32, row_count)
    local_energy = row_ids // (2 * groups)
    component = row_ids // groups % 2
    source = row_ids % groups
    stored = source * per_device + local_energy
    grid_point = energy_index[stored]
    frequency = lax.iota(jnp.int32, padded_len)
    forward_phase = frequency[:, None] * grid_point[None, :] % padded_len
    forward_angle = forward_phase.astype(jnp.float32) * (2.0 * math.pi / padded_len)
    cos_fwd = jnp.cos(forward_angle)
    sin_fwd = jnp.sin(forward_angle)
    real_column = (component == 0)[None, :]
    forward = jnp.concatenate(
        [jnp.where(real_column, cos_fwd, sin_fwd), jnp.where(real_column, -sin_fwd, cos_fwd)],
        axis=0,
    )
    shifted = grid_point + grid_size // 2
    backward_phase = shifted[:, None] * frequency[None, :] % padded_len
    backward_angle = backward_phase.astype(jnp.float32) * (2.0 * math.pi / padded_len)
    cos_back = jnp.cos(backward_angle)
    sin_back = jnp.sin(backward_angle)
    real_row = (component == 0)[:, None]
    factor = grid_size ** (-0.5) / padded_len
    left_half = jnp.where(real_row, -sin_back, cos_back) * factor
    right_half = jnp.where(real_row, -cos_back, -sin_back) * factor
    backward = jnp.concatenate([left_half, right_half], axis=1)
    return (forward, backward)


def transform(matrix_high, matrix_low, operand):
    return jnp.dot(matrix_high, operand, preferred_element_type=jnp.float32) + jnp.dot(
        matrix_low, operand, preferred_element_type=jnp.float32
    )


def convolve(green_rows, screen_rows, forward, backward):
    padded_len = forward.shape[0] // 2
    forward_high = forward.astype(jnp.bfloat16)
    forward_low = (forward - forward_high.astype(jnp.float32)).astype(jnp.bfloat16)
    green_hat = transform(forward_high, forward_low, green_rows)
    screen_hat = transform(forward_high, forward_low, screen_rows)
    green_real = green_hat[:padded_len]
    green_imag = green_hat[padded_len:]
    screen_real = screen_hat[:padded_len]
    screen_imag = screen_hat[padded_len:]
    prod_real = green_real * screen_real - green_imag * screen_imag
    prod_imag = green_real * screen_imag + green_imag * screen_real
    merged = jnp.concatenate([prod_real, prod_imag], axis=0)
    return jnp.dot(backward, merged, precision=lax.Precision.HIGH).astype(jnp.bfloat16)


def shards(g_lesser, w_lesser, g_retarded, energy_index):
    energies_here = g_lesser.shape[0]
    width = g_lesser.shape[3]
    groups = lax.axis_size("energy")
    forward, backward = twiddles(energy_index, energies_here, groups)
    own_row = g_retarded[:, :, 0]
    columns = width * width // groups
    green = g_lesser.reshape(energies_here, 2, groups, columns)
    screen = w_lesser.reshape(energies_here, 2, groups, columns)
    green_el, screen_el = (
        lax.all_to_all(green, "energy", split_axis=2, concat_axis=2, tiled=True),
        lax.all_to_all(screen, "energy", split_axis=2, concat_axis=2, tiled=True),
    )
    sigma_el = convolve(
        green_el.reshape(-1, columns), screen_el.reshape(-1, columns), forward, backward
    )
    sigma_el = sigma_el.reshape(energies_here, 2, groups, columns)
    sigma_back = lax.all_to_all(sigma_el, "energy", split_axis=2, concat_axis=2, tiled=True)
    sigma_lesser = sigma_back.reshape(energies_here, 2, 1, width, width)
    first_prod = jnp.einsum(
        "ecnij,ednjl->encdil",
        own_row,
        lax.all_gather(sigma_lesser, "space", axis=2, tiled=True),
        preferred_element_type=jnp.float32,
    )
    left_product = jnp.stack(
        [
            first_prod[:, :, 0, 0] - first_prod[:, :, 1, 1],
            first_prod[:, :, 0, 1] + first_prod[:, :, 1, 0],
        ],
        axis=1,
    ).astype(jnp.bfloat16)
    second_prod = jnp.einsum(
        "ecnil,ednml->ecdim", left_product, own_row, preferred_element_type=jnp.float32
    )
    out_real = second_prod[:, 0, 0] + second_prod[:, 1, 1]
    out_imag = second_prod[:, 1, 0] - second_prod[:, 0, 1]
    delta = jnp.stack([out_real, out_imag], axis=1)
    delta_green = delta.astype(jnp.bfloat16).reshape(energies_here, 2, 1, width, width)
    return (sigma_lesser, delta_green)


def solution(mesh):
    return jax.shard_map(
        shards,
        mesh=mesh,
        in_specs=(
            P("energy", None, "space", None, None),
            P("energy", None, "space", None, None),
            P("energy", None, "space", None, None, None),
            P(),
        ),
        out_specs=(P("energy", None, "space", None, None), P("energy", None, "space", None, None)),
        check_vma=False,
    )
```

profile of v0, /device:TPU:1, one launch (start us, length us, event | category | flops | bytes accessed | tf_op | source)
XLA Modules:
  0.0 215.1 jit_solution(1046797866290290498)
XLA Ops:
  7.2 1.6 reshape.274
  8.8 2.1 copy.28
  10.9 15.1 %all-to-all-start.1 = ((bf16[1,2,64,4096]{3,1,0,2:T(2,128)(2,1)}), bf16[1,2,64,4096]{3,1,0,2:T(2,128)(2,1)S(1)}, u32[]{:S(2)}, u32[]{:S(2)}) async-start(bf16[1,2,64,4096]{3,1,0,2:T(2,128)(2,1)} %copy.28), calls=%async_computation.1 | async-start | bytes 2097152 | tf_op jit(solution)/shard_map/all_to_all | solution.py:74
  26.6 2.1 copy.26
  28.6 25.1 %all-to-all-done.1 = bf16[1,2,64,4096]{3,1,0,2:T(2,128)(2,1)S(1)} async-done(((bf16[1,2,64,4096]{3,1,0,2:T(2,128)(2,1)}), bf16[1,2,64,4096]{3,1,0,2:T(2,128)(2,1)S(1)}, u32[]{:S(2)}, u32[]{:S(2)}) %all-to-all-start.1) | async-done | bytes 1048608 | tf_op jit(solution)/shard_map/all_to_all | solution.py:74
  53.7 8.3 %all-to-all-start = ((bf16[1,2,64,4096]{3,1,0,2:T(2,128)(2,1)}), bf16[1,2,64,4096]{3,1,0,2:T(2,128)(2,1)S(1)}, u32[]{:S(2)}, u32[]{:S(2)}) async-start(bf16[1,2,64,4096]{3,1,0,2:T(2,128)(2,1)} %copy.26), calls=%async_computation | async-start | bytes 2097152 | tf_op jit(solution)/shard_map/all_to_all | solution.py:73
  62.3 1.2 gather_fusion
  64.8 0.7 fusion.36
  65.5 2.6 %convolution_add_fusion = f32[256,4096]{1,0:T(8,128)} fusion(f32[256,4096]{1,0:T(8,128)S(1)} %fusion.36, bf16[128,4096]{1,0:T(8,128)(2,1)S(1)} %bitcast.74, f32[128,128]{1,0:T(8,128)S(1)} %get-tuple-element.18, f32[128,128]{1,0:T(8,128)S(1)} %get-tuple-element.19), kind=kOutput, calls=%fused_computation.2 | convolution fusion | flops 269647872 | bytes 9568256 | tf_op jit(solution)/shard_map/dot_general | solution.py:42
  68.1 22.7 %all-to-all-done = bf16[1,2,64,4096]{3,1,0,2:T(2,128)(2,1)S(1)} async-done(((bf16[1,2,64,4096]{3,1,0,2:T(2,128)(2,1)}), bf16[1,2,64,4096]{3,1,0,2:T(2,128)(2,1)S(1)}, u32[]{:S(2)}, u32[]{:S(2)}) %all-to-all-start) | async-done | bytes 1048608 | tf_op jit(solution)/shard_map/all_to_all | solution.py:73
  91.3 0.7 fusion.38
  92.0 0.7 convolution_add_fusion.1
  92.8 1.5 copy-done.2
  94.2 0.9 multiply_subtract_fusion
  95.2 1.5 convolution_convert_fusion
  96.7 1.1 copy.30
  97.8 32.1 %all_to_all.15 = bf16[1,2,64,4096]{3,1,0,2:T(2,128)(2,1)S(1)} all-to-all(bf16[1,2,64,4096]{3,1,0,2:T(2,128)(2,1)S(1)} %copy.30), channel_id=1, replica_groups=mesh['energy'=64,'space'=4] {'energy'}, dimensions={2} | all-to-all | bytes 2097152 | tf_op jit(solution)/shard_map/all_to_all | solution.py:80
  130.6 1.3 reshape.277
  131.9 47.4 %all-gather.2.cloned.1.call-done = bf16[1,2,4,512,512]{4,3,1,0,2:T(8,128)(2,1)} async-done(((bf16[1,2,1,512,512]{4,3,1,0,2:T(8,128)(2,1)}), bf16[1,2,4,512,512]{4,3,1,0,2:T(8,128)(2,1)}) %all-gather.2.cloned.1.call-update) | async-done | bytes 4194320 | tf_op jit(solution)/shard_map/all_gather | solution.py:85
  179.3 14.1 %convolution_bitcast_fusion = f32[1,4,2,2,512,512]{4,5,2,3,1,0:T(8,128)} fusion(bf16[1,2,4,512,512]{4,3,1,0,2:T(8,128)(2,1)} %all-gather.2.cloned.1.call-done, bf16[1,2,1,4,512,512]{5,4,3,2,1,0:T(8,128)(2,1)} %param.6), kind=kOutput, calls=%fused_computation.1 | convolution fusion | flops 4294967296 | bytes 25165824 | tf_op jit(solution)/shard_map/ecnij,ednjl->encdil/dot_general | solution.py:82
  193.4 4.2 %fusion.13 = bf16[1,4,512,512]{2,3,1,0:T(8,128)(2,1)S(1)} fusion(f32[1,4,2,2,512,512]{4,5,2,3,1,0:T(8,128)} %convolution_bitcast_fusion), kind=kLoop, calls=%fused_computation.22 | loop fusion | flops 2097152 | bytes 10485760 | tf_op jit(solution)/shard_map/add | solution.py:91
  197.6 4.4 %fusion.12 = bf16[1,4,512,512]{2,3,1,0:T(8,128)(2,1)S(1)} fusion(f32[1,4,2,2,512,512]{4,5,2,3,1,0:T(8,128)} %convolution_bitcast_fusion), kind=kLoop, calls=%fused_computation.21 | loop fusion | flops 2097152 | bytes 10485760 | tf_op jit(solution)/shard_map/sub | solution.py:90
  202.3 4.5 %fusion.11 = f32[1,2,2,512,512]{4,3,2,1,0:T(8,128)S(1)} fusion(bf16[1,4,512,512]{2,3,1,0:T(8,128)(2,1)S(1)} %fusion.13, bf16[1,4,512,512]{2,3,1,0:T(8,128)(2,1)S(1)} %fusion.12, bf16[1,2,1,4,512,512]{5,4,3,2,1,0:T(8,128)(2,1)S(1)} %copy-done.3), kind=kOutput, calls=%fused_computation.20 | convolution fusion | flops 4303355904 | bytes 12582912 | tf_op jit(solution)/shard_map/ecnil,ednml->ecdim/dot_general | solution.py:95
  207.2 1.1 pad_maximum_fusion
  (21 shorter events, 3.7 us)
Async XLA Ops:
  7.2 55.1 %copy-start = (s32[64]{0:T(128)S(1)}, s32[64]{0:T(128)}, u32[]{:S(2)}) copy-start(s32[64]{0:T(128)} %param.7) | copy-start | bytes 772
  7.2 18.8 %copy-start.4 = (bf16[1,2,1,512,512]{4,3,2,1,0:T(8,128)(2,1)S(1)}, bf16[1,2,1,512,512]{4,3,2,1,0:T(8,128)(2,1)}, u32[]{:S(2)}) copy-start(bf16[1,2,1,512,512]{4,3,2,1,0:T(8,128)(2,1)} %param.4) | copy-start | bytes 3145732
  10.9 42.8 %all-to-all-start.1 = ((bf16[1,2,64,4096]{3,1,0,2:T(2,128)(2,1)}), bf16[1,2,64,4096]{3,1,0,2:T(2,128)(2,1)S(1)}, u32[]{:S(2)}, u32[]{:S(2)}) async-start(bf16[1,2,64,4096]{3,1,0,2:T(2,128)(2,1)} %copy.28), calls=%async_computation.1 | async-start | bytes 2097152 | tf_op jit(solution)/shard_map/all_to_all | solution.py:74
  53.7 37.0 %all-to-all-start = ((bf16[1,2,64,4096]{3,1,0,2:T(2,128)(2,1)}), bf16[1,2,64,4096]{3,1,0,2:T(2,128)(2,1)S(1)}, u32[]{:S(2)}, u32[]{:S(2)}) async-start(bf16[1,2,64,4096]{3,1,0,2:T(2,128)(2,1)} %copy.26), calls=%async_computation | async-start | bytes 2097152 | tf_op jit(solution)/shard_map/all_to_all | solution.py:73
  62.0 117.3 %all-gather.2.cloned.1.call-start = ((), (), s32[]{:S(2)}) async-start(), calls=%async_computation.3 | async-start | bytes 5242880 | tf_op jit(solution)/shard_map/all_gather | solution.py:85
  92.0 2.2 %copy-start.2 = (f32[256,4096]{1,0:T(8,128)S(1)}, f32[256,4096]{1,0:T(8,128)}, u32[]{:S(2)}) copy-start(f32[256,4096]{1,0:T(8,128)} %convolution_add_fusion) | copy-start | bytes 12582916
  197.6 4.6 %copy-start.3 = (bf16[1,2,1,4,512,512]{5,4,3,2,1,0:T(8,128)(2,1)S(1)}, bf16[1,2,1,4,512,512]{5,4,3,2,1,0:T(8,128)(2,1)}, u32[]{:S(2)}) copy-start(bf16[1,2,1,4,512,512]{5,4,3,2,1,0:T(8,128)(2,1)} %param.6) | copy-start | bytes 12582916
  202.3 6.0 %copy-start.1 = (s32[64]{0:T(128)S(1)}, s32[64]{0:T(128)}, u32[]{:S(2)}) copy-start(s32[64]{0:T(128)} %param.7) | copy-start | bytes 772
Sparse Core Ops, SparseCore 0:
  132.0 47.2 all-gather.1
where the time goes:
time: 215 us
  waiting for transfers between devices  95.2 us (44%)
  blocking collectives  32.1 us (15%)
  matrix products  24.9 us (12%)
  starting transfers between devices  23.7 us (11%)
  between operations  14.2 us (7%)
  local copies, waits for them, and re-layouts  13.4 us (6%)
  other arithmetic  11.6 us (5%)
    all_gather x1, waiting for transfers between devices, shards(): lax.all_gather(sigma_lesser, 'space', axis=2, tiled=True)  47.4 us
    all_to_all x1, blocking collectives, shards(): lax.all_to_all(sigma_el, 'energy', split_axis=2, concat_axis=2, tiled=True)  32.1 us
    all_to_all x1, waiting for transfers between devices, shards(): lax.all_to_all(screen, 'energy', split_axis=2, concat_axis=2, tiled=True)  25.1 us
    all_to_all x1, waiting for transfers between devices, shards(): lax.all_to_all(green, 'energy', split_axis=2, concat_axis=2, tiled=True)  22.7 us
    all_to_all x1, starting transfers between devices, shards(): lax.all_to_all(screen, 'energy', split_axis=2, concat_axis=2, tiled=True)  15.1 us
    dot_general x1, matrix products, shards(): jnp.einsum('ecnij,ednjl->encdil', own_row, lax.all_gather(sigma_lesser, '...  14.1 us
    all_to_all x1, starting transfers between devices, shards(): lax.all_to_all(green, 'energy', split_axis=2, concat_axis=2, tiled=True)  8.33 us
    dot_general x1, matrix products, shards(): jnp.einsum('ecnil,ednml->ecdim', left_product, own_row, preferred_element...  4.54 us
  transfers between devices with their start and end apart: 3, of which 3 were waited for; matrix products, arithmetic and copies ran while one was open for 4% of the time, Pallas kernels for 0%

commit v1 on v0

--- a/solution.py
+++ b/solution.py
@@ -82,7 +82,10 @@
     first_prod = jnp.einsum(
         "ecnij,ednjl->encdil",
         own_row,
-        lax.all_gather(sigma_lesser, "space", axis=2, tiled=True),
+        jnp.concatenate(
+            lax.all_to_all(jnp.stack([sigma_lesser] * lax.axis_size("space")), "space", 0, 0),
+            axis=2,
+        ),
         preferred_element_type=jnp.float32,
     )
     left_product = jnp.stack(

time: 215 us -> 201 us (0.935)
  between operations: 14.2 us -> 0.85 us
  starting transfers between devices: 23.7 us -> 32.1 us
  other arithmetic: 11.6 us -> 4.62 us
  matrix products: 24.9 us -> 18.4 us
  local copies, waits for them, and re-layouts: 13.4 us -> 17.9 us
    all_gather x1 -> x0, waiting for transfers between devices: 47.4 us -> none  [shards(): lax.all_gather(sigma_lesser, 'space', axis=2, tiled=True)]
    all_to_all x0 -> x1, waiting for transfers between devices: none -> 45.6 us  [shards(): lax.all_to_all(jnp.stack([sigma_lesser] * lax.axis_size('space')), 'space...]
    all_to_all x0 -> x1, starting transfers between devices: none -> 8.45 us  [shards(): lax.all_to_all(jnp.stack([sigma_lesser] * lax.axis_size('space')), 'space...]
    dot_general x1, matrix products: 14.1 us -> 7.61 us  [shards(): jnp.einsum('ecnij,ednjl->encdil', own_row, jnp.concatenate(lax.all_to_all...]
    sub x1, other arithmetic: 4.42 us -> 0.89 us  [shards(): first_prod[:, :, 0, 0] - first_prod[:, :, 1, 1]]
    add x1, other arithmetic: 4.19 us -> 0.75 us  [shards(): first_prod[:, :, 0, 1] + first_prod[:, :, 1, 0]]
    another operation x0 -> x3, local copies, waits for them, and re-layouts: none -> 3.42 us  [shards(): jnp.stack([sigma_lesser] * lax.axis_size('space'))]
  transfers between devices with their start and end apart: 3 -> 3, of which waited for: 3 -> 3; matrix products, arithmetic and copies ran while one was open for 4% -> 5% of each run, Pallas kernels for 0% -> 0%
where the time goes in v1:
time: 201 us; the launch traced here: 199 us
  waiting for transfers between devices  93.3 us (46%)
  starting transfers between devices  32.1 us (16%)
  blocking collectives  32.1 us (16%)
  matrix products  18.4 us (9%)
  local copies, waits for them, and re-layouts  17.9 us (9%)
  other arithmetic  4.62 us (2%)
    all_to_all x1, waiting for transfers between devices, shards(): lax.all_to_all(jnp.stack([sigma_lesser] * lax.axis_size('space')), 'space...  45.6 us
    all_to_all x1, blocking collectives, shards(): lax.all_to_all(sigma_el, 'energy', split_axis=2, concat_axis=2, tiled=True)  32.1 us
    all_to_all x1, waiting for transfers between devices, shards(): lax.all_to_all(screen, 'energy', split_axis=2, concat_axis=2, tiled=True)  25.1 us
    all_to_all x1, waiting for transfers between devices, shards(): lax.all_to_all(green, 'energy', split_axis=2, concat_axis=2, tiled=True)  22.7 us
    all_to_all x1, starting transfers between devices, shards(): lax.all_to_all(screen, 'energy', split_axis=2, concat_axis=2, tiled=True)  15.1 us
    all_to_all x1, starting transfers between devices, shards(): lax.all_to_all(green, 'energy', split_axis=2, concat_axis=2, tiled=True)  8.51 us
    all_to_all x1, starting transfers between devices, shards(): lax.all_to_all(jnp.stack([sigma_lesser] * lax.axis_size('space')), 'space...  8.45 us
    dot_general x1, matrix products, shards(): jnp.einsum('ecnij,ednjl->encdil', own_row, jnp.concatenate(lax.all_to_all...  7.61 us
  transfers between devices with their start and end apart: 3, of which 3 were waited for; matrix products, arithmetic and copies ran while one was open for 5% of the time, Pallas kernels for 0%

profile of v1, /device:TPU:1, one launch (start us, length us, event | category | flops | bytes accessed | tf_op | source)
XLA Modules:
  0.0 199.3 jit_solution(15464339068481596458)
XLA Ops:
  0.7 1.6 reshape.283
  2.3 2.1 %copy.24 = bf16[1,2,64,4096]{3,1,0,2:T(2,128)(2,1)} copy(bf16[1,2,64,4096]{3,2,1,0:T(8,128)(2,1)S(1)} %reshape.283) | data formatting | bytes 2097152 | tf_op jit(solution)/shard_map/reshape | solution.py:71
  4.4 15.1 %all-to-all-start.1 = ((bf16[1,2,64,4096]{3,1,0,2:T(2,128)(2,1)}), bf16[1,2,64,4096]{3,1,0,2:T(2,128)(2,1)S(1)}, u32[]{:S(2)}, u32[]{:S(2)}) async-start(bf16[1,2,64,4096]{3,1,0,2:T(2,128)(2,1)} %copy.24), calls=%async_computation.1 | async-start | bytes 2097152 | tf_op jit(solution)/shard_map/all_to_all | solution.py:74
  20.0 2.1 %copy.22 = bf16[1,2,64,4096]{3,1,0,2:T(2,128)(2,1)} copy(bf16[1,2,64,4096]{3,2,1,0:T(8,128)(2,1)S(1)} %reshape.281) | data formatting | bytes 2097152 | tf_op jit(solution)/shard_map/reshape | solution.py:70
  22.1 25.1 %all-to-all-done.1 = bf16[1,2,64,4096]{3,1,0,2:T(2,128)(2,1)S(1)} async-done(((bf16[1,2,64,4096]{3,1,0,2:T(2,128)(2,1)}), bf16[1,2,64,4096]{3,1,0,2:T(2,128)(2,1)S(1)}, u32[]{:S(2)}, u32[]{:S(2)}) %all-to-all-start.1) | async-done | bytes 1048608 | tf_op jit(solution)/shard_map/all_to_all | solution.py:74
  47.2 8.5 %all-to-all-start = ((bf16[1,2,64,4096]{3,1,0,2:T(2,128)(2,1)}), bf16[1,2,64,4096]{3,1,0,2:T(2,128)(2,1)S(1)}, u32[]{:S(2)}, u32[]{:S(2)}) async-start(bf16[1,2,64,4096]{3,1,0,2:T(2,128)(2,1)} %copy.22), calls=%async_computation | async-start | bytes 2097152 | tf_op jit(solution)/shard_map/all_to_all | solution.py:73
  55.7 1.2 gather_fusion
  58.9 2.6 %convolution_add_fusion = f32[256,4096]{1,0:T(8,128)} fusion(f32[256,4096]{1,0:T(8,128)S(1)} %fusion.36, bf16[128,4096]{1,0:T(8,128)(2,1)S(1)} %bitcast.79, f32[128,128]{1,0:T(8,128)S(1)} %get-tuple-element.12, f32[128,128]{1,0:T(8,128)S(1)} %get-tuple-element.13), kind=kOutput, calls=%fused_computation.2 | convolution fusion | flops 269647872 | bytes 9568256 | tf_op jit(solution)/shard_map/dot_general | solution.py:42
  61.5 22.7 %all-to-all-done = bf16[1,2,64,4096]{3,1,0,2:T(2,128)(2,1)S(1)} async-done(((bf16[1,2,64,4096]{3,1,0,2:T(2,128)(2,1)}), bf16[1,2,64,4096]{3,1,0,2:T(2,128)(2,1)S(1)}, u32[]{:S(2)}, u32[]{:S(2)}) %all-to-all-start) | async-done | bytes 1048608 | tf_op jit(solution)/shard_map/all_to_all | solution.py:73
  86.2 1.5 copy-done.2
  87.7 0.9 multiply_subtract_fusion
  88.6 1.5 convolution_convert_fusion
  90.2 1.1 copy.26
  91.3 32.1 %all_to_all.20 = bf16[1,2,64,4096]{3,1,0,2:T(2,128)(2,1)S(1)} all-to-all(bf16[1,2,64,4096]{3,1,0,2:T(2,128)(2,1)S(1)} %copy.26), channel_id=1, replica_groups=mesh['energy'=64,'space'=4] {'energy'}, dimensions={2} | all-to-all | bytes 2097152 | tf_op jit(solution)/shard_map/all_to_all | solution.py:80
  125.1 2.3 %stack.6 = bf16[4,1,2,1,512,512]{4,5,2,3,1,0:T(8,128)(2,1)} broadcast(bf16[2,512,512]{1,2,0:T(8,128)(2,1)S(1)} %copy.29), dimensions={2,4,5} | broadcast | bytes 5242880 | tf_op jit(solution)/shard_map/stack | solution.py:86
  127.5 8.5 %all-to-all-start.3 = ((bf16[4,1,2,1,512,512]{4,5,2,3,1,0:T(8,128)(2,1)}), bf16[4,1,2,1,512,512]{4,5,2,3,1,0:T(8,128)(2,1)}, u32[]{:S(2)}, u32[]{:S(2)}) async-start(bf16[4,1,2,1,512,512]{4,5,2,3,1,0:T(8,128)(2,1)} %stack.6), calls=%async_computation.3 | async-start | bytes 8388608 | tf_op jit(solution)/shard_map/all_to_all | solution.py:86
  135.9 1.3 reshape.286
  137.2 45.6 %all-to-all-done.3 = bf16[4,1,2,1,512,512]{4,5,2,3,1,0:T(8,128)(2,1)} async-done(((bf16[4,1,2,1,512,512]{4,5,2,3,1,0:T(8,128)(2,1)}), bf16[4,1,2,1,512,512]{4,5,2,3,1,0:T(8,128)(2,1)}, u32[]{:S(2)}, u32[]{:S(2)}) %all-to-all-start.3) | async-done | bytes 4194336 | tf_op jit(solution)/shard_map/all_to_all | solution.py:86
  182.8 7.6 %convolution_bitcast_fusion = f32[1,4,2,2,512,512]{4,5,2,3,1,0:T(8,128)S(1)} fusion(bf16[4,1,2,1,512,512]{4,5,2,3,1,0:T(8,128)(2,1)} %all-to-all-done.3, bf16[1,2,1,4,512,512]{5,4,3,2,1,0:T(8,128)(2,1)} %param.6), kind=kOutput, calls=%fused_computation.1 | convolution fusion | flops 4294967296 | bytes 25165824 | tf_op jit(solution)/shard_map/ecnij,ednjl->encdil/dot_general | solution.py:82
  190.4 0.8 fusion.13
  191.1 0.9 fusion.12
  192.0 1.3 copy-done.3
  193.3 4.5 %fusion.11 = f32[1,2,2,512,512]{4,3,2,1,0:T(8,128)S(1)} fusion(bf16[1,4,512,512]{2,3,1,0:T(8,128)(2,1)S(1)} %fusion.13, bf16[1,4,512,512]{2,3,1,0:T(8,128)(2,1)S(1)} %fusion.12, bf16[1,2,1,4,512,512]{5,4,3,2,1,0:T(8,128)(2,1)S(1)} %copy-done.3), kind=kOutput, calls=%fused_computation.20 | convolution fusion | flops 4303355904 | bytes 12582912 | tf_op jit(solution)/shard_map/ecnil,ednml->ecdim/dot_general | solution.py:98
  198.2 1.1 pad_maximum_fusion
  (23 shorter events, 6.4 us)
Async XLA Ops:
  0.6 55.1 %copy-start = (s32[64]{0:T(128)S(1)}, s32[64]{0:T(128)}, u32[]{:S(2)}) copy-start(s32[64]{0:T(128)} %param.7) | copy-start | bytes 772
  0.6 18.8 %copy-start.4 = (bf16[1,2,1,512,512]{4,3,2,1,0:T(8,128)(2,1)S(1)}, bf16[1,2,1,512,512]{4,3,2,1,0:T(8,128)(2,1)}, u32[]{:S(2)}) copy-start(bf16[1,2,1,512,512]{4,3,2,1,0:T(8,128)(2,1)} %param.4) | copy-start | bytes 3145732
  4.4 42.8 %all-to-all-start.1 = ((bf16[1,2,64,4096]{3,1,0,2:T(2,128)(2,1)}), bf16[1,2,64,4096]{3,1,0,2:T(2,128)(2,1)S(1)}, u32[]{:S(2)}, u32[]{:S(2)}) async-start(bf16[1,2,64,4096]{3,1,0,2:T(2,128)(2,1)} %copy.24), calls=%async_computation.1 | async-start | bytes 2097152 | tf_op jit(solution)/shard_map/all_to_all | solution.py:74
  47.2 37.0 %all-to-all-start = ((bf16[1,2,64,4096]{3,1,0,2:T(2,128)(2,1)}), bf16[1,2,64,4096]{3,1,0,2:T(2,128)(2,1)S(1)}, u32[]{:S(2)}, u32[]{:S(2)}) async-start(bf16[1,2,64,4096]{3,1,0,2:T(2,128)(2,1)} %copy.22), calls=%async_computation | async-start | bytes 2097152 | tf_op jit(solution)/shard_map/all_to_all | solution.py:73
  85.5 2.2 %copy-start.2 = (f32[256,4096]{1,0:T(8,128)S(1)}, f32[256,4096]{1,0:T(8,128)}, u32[]{:S(2)}) copy-start(f32[256,4096]{1,0:T(8,128)} %convolution_add_fusion) | copy-start | bytes 12582916
  127.5 55.3 %all-to-all-start.3 = ((bf16[4,1,2,1,512,512]{4,5,2,3,1,0:T(8,128)(2,1)}), bf16[4,1,2,1,512,512]{4,5,2,3,1,0:T(8,128)(2,1)}, u32[]{:S(2)}, u32[]{:S(2)}) async-start(bf16[4,1,2,1,512,512]{4,5,2,3,1,0:T(8,128)(2,1)} %stack.6), calls=%async_computation.3 | async-start | bytes 8388608 | tf_op jit(solution)/shard_map/all_to_all | solution.py:86
  191.1 2.2 %copy-start.3 = (bf16[1,2,1,4,512,512]{5,4,3,2,1,0:T(8,128)(2,1)S(1)}, bf16[1,2,1,4,512,512]{5,4,3,2,1,0:T(8,128)(2,1)}, u32[]{:S(2)}) copy-start(bf16[1,2,1,4,512,512]{5,4,3,2,1,0:T(8,128)(2,1)} %param.6) | copy-start | bytes 12582916
  193.3 6.0 %copy-start.1 = (s32[64]{0:T(128)S(1)}, s32[64]{0:T(128)}, u32[]{:S(2)}) copy-start(s32[64]{0:T(128)} %param.7) | copy-start | bytes 772
